TPU v7x, 256 devices: a whole 4x4x8 slice. The times are simulated.
256 devices in a mesh: dp: 4 (over y), expert: 64 (over x, z, core).
Axes of the slice: x: 4, y: 4, z: 8, core: 2. Of those that a mesh axis runs over, the one named last changes fastest.
Arguments:
- tokens: bfloat16 [8192, 4096], P('expert', 'dp'), may hold values from -6 to 6
- cotangent: bfloat16 [8192, 4096], P('expert', 'dp'), may hold values from -1.5 to 1.5
- router_probs: bfloat16 [8192, 8], P('expert'), may hold values from 0.049804688 to 1
- expert_ids: int32 [8192, 8], P('expert'), may hold values from 0 to 63, all different within a row; in each aligned block of 128 rows (0 to 127, 128 to 255, ...) at most 17 rows name the same one
- w_gate: bfloat16 [64, 768, 4096], P('expert', None, 'dp'), may hold values from -0.09375 to 0.09375
- w_up: bfloat16 [64, 768, 4096], P('expert', None, 'dp'), may hold values from -0.09375 to 0.09375
- w_down: bfloat16 [64, 768, 4096], P('expert', None, 'dp'), may hold values from -0.21875 to 0.21875
Outputs:
- token_grads: bfloat16 [8192, 4096], P('expert', 'dp')
- prob_grads: float32 [8192, 8], P('expert')
- gate_grads: bfloat16 [64, 768, 4096], P('expert', None, 'dp')
- up_grads: bfloat16 [64, 768, 4096], P('expert', None, 'dp')
- down_grads: bfloat16 [64, 768, 4096], P('expert', None, 'dp')
Inputs may be any that keep to these rules, and one draw needn't show every extreme that they name: `expert_ids`: each row names 8 different experts. Among the 128 tokens of one index of expert no expert is named more than 17 times, a bound that some block reaches.
All inputs are finite; a program needn't handle non-finite values.
Results may differ from a plain program's by a relative error of at most 0.02.
Values may be sent and summed in bfloat16 or wider, within the bound.
A program may use at most 128 MiB of HBM per device.

v0:
```python
import jax
import jax.numpy as jnp
from jax import lax
from jax.sharding import PartitionSpec as P


def contract_last(left_matrix, right_matrix):
    return lax.dot_general(
        left_matrix, right_matrix, (((1,), (1,)), ((), ())), preferred_element_type=jnp.float32
    )


def contract_first(left_matrix, right_matrix):
    return lax.dot_general(
        left_matrix, right_matrix, (((0,), (0,)), ((), ())), preferred_element_type=jnp.float32
    )


def activations(gate_value, up_value, back_value, weights):
    sigmoid_gate = jax.nn.sigmoid(gate_value)
    silu_gate = gate_value * sigmoid_gate
    hidden = (silu_gate * up_value).astype(jnp.bfloat16)
    prob_local = jnp.sum(hidden.astype(jnp.float32) * back_value, axis=1)
    grad_back = weights[:, None] * back_value
    grad_gate = (
        grad_back * up_value * sigmoid_gate * (1.0 + gate_value * (1.0 - sigmoid_gate))
    ).astype(jnp.bfloat16)
    grad_up = (grad_back * silu_gate).astype(jnp.bfloat16)
    return (hidden, grad_gate, grad_up, prob_local)


def local(tokens, cotangent, router_probs, expert_ids, w_gate, w_up, w_down):
    experts = lax.axis_size("expert")
    local_tokens, top_count = expert_ids.shape
    row_count = local_tokens * top_count
    slot_count = min(local_tokens, max(2, (row_count + experts - 1) // experts * 17 // 16))
    features = tokens.shape[1]
    flat_ids = expert_ids.reshape(-1)
    hit_table = (flat_ids[:, None] == jnp.arange(experts, dtype=jnp.int32)[None, :]).astype(
        jnp.int32
    )
    slot_ranks = jnp.sum(jnp.cumsum(hit_table, axis=0) * hit_table, axis=1) - 1
    slot_places = flat_ids * slot_count + slot_ranks
    slot_table = jnp.full((experts * slot_count,), row_count, jnp.int32)
    slot_table = slot_table.at[slot_places].set(jnp.arange(row_count, dtype=jnp.int32))
    filled = slot_table < row_count
    sources = jnp.minimum(slot_table, row_count - 1)
    owners = sources // top_count
    send_probs = jnp.where(
        filled, router_probs.reshape(-1)[sources], jnp.zeros((), router_probs.dtype)
    )
    send_probs = send_probs.reshape(experts, slot_count)

    def pack_rows(source):
        picked = jnp.where(filled[:, None], source[owners], jnp.zeros((), source.dtype))
        return picked.reshape(experts, slot_count, source.shape[1])

    recv_in, recv_grad, recv_probs = (
        lax.all_to_all(pack_rows(tokens), "expert", split_axis=0, concat_axis=0, tiled=True),
        lax.all_to_all(pack_rows(cotangent), "expert", split_axis=0, concat_axis=0, tiled=True),
        lax.all_to_all(send_probs, "expert", split_axis=0, concat_axis=0, tiled=True),
    )
    inputs = recv_in.reshape(experts * slot_count, features)
    grads_in = recv_grad.reshape(experts * slot_count, features)
    weights = recv_probs.reshape(-1).astype(jnp.float32)
    weight_gate = w_gate[0]
    weight_up = w_up[0]
    weight_down = w_down[0]
    gate_part = contract_last(inputs, weight_gate)
    up_part = contract_last(inputs, weight_up)
    back_part = contract_last(grads_in, weight_down)
    gate_value, up_value, back_value = (
        lax.psum(gate_part.astype(jnp.bfloat16), "dp").astype(jnp.float32),
        lax.psum(up_part.astype(jnp.bfloat16), "dp").astype(jnp.float32),
        lax.psum(back_part.astype(jnp.bfloat16), "dp").astype(jnp.float32),
    )
    hidden, grad_gate, grad_up, prob_value = activations(gate_value, up_value, back_value, weights)
    scaled = (weights[:, None] * grads_in).astype(jnp.bfloat16)
    row_term = jnp.dot(grad_gate, weight_gate, preferred_element_type=jnp.float32)
    row_term = (row_term + jnp.dot(grad_up, weight_up, preferred_element_type=jnp.float32)).astype(
        jnp.bfloat16
    )
    gate_grad = contract_first(grad_gate, inputs).astype(jnp.bfloat16)
    up_grad = contract_first(grad_up, inputs).astype(jnp.bfloat16)
    down_grad = contract_first(hidden, scaled).astype(jnp.bfloat16)
    back_terms, back_probs = (
        lax.all_to_all(
            row_term.reshape(experts, slot_count, features),
            "expert",
            split_axis=0,
            concat_axis=0,
            tiled=True,
        ),
        lax.all_to_all(
            prob_value.astype(jnp.bfloat16).reshape(experts, slot_count),
            "expert",
            split_axis=0,
            concat_axis=0,
            tiled=True,
        ),
    )
    returned = back_terms.reshape(experts * slot_count, features)[slot_places].astype(jnp.float32)
    token_sum = jnp.sum(returned.reshape(local_tokens, top_count, features), axis=1)
    prob_grads = (
        back_probs.reshape(-1)[slot_places].astype(jnp.float32).reshape(local_tokens, top_count)
    )
    return (
        token_sum.astype(jnp.bfloat16),
        prob_grads,
        gate_grad[None],
        up_grad[None],
        down_grad[None],
    )


def solution(mesh):
    return jax.shard_map(
        local,
        mesh=mesh,
        in_specs=(
            P("expert", "dp"),
            P("expert", "dp"),
            P("expert", None),
            P("expert", None),
            P("expert", None, "dp"),
            P("expert", None, "dp"),
            P("expert", None, "dp"),
        ),
        out_specs=(
            P("expert", "dp"),
            P("expert", None),
            P("expert", None, "dp"),
            P("expert", None, "dp"),
            P("expert", None, "dp"),
        ),
        check_vma=False,
    )
```

profile of v0, /device:TPU:1, one launch (start us, length us, event | category | flops | bytes accessed | tf_op | source)
XLA Modules:
  0.0 482.7 jit_solution(12835714948182964482)
XLA Ops:
  10.1 18.0 %reduce-window.6 = s32[64,8,128]{2,1,0:T(8,128)S(1)} reduce-window(s32[64,8,128]{2,1,0:T(8,128)S(1)} %fusion.26, s32[]{:T(128)} %constant.16.clone.1), window={size=1x1x128 pad=0_0x0_0x127_0}, to_apply=%region_0.0 | reduce-window | flops 8323072 | bytes 524292 | tf_op jit(solution)/shard_map/reduce-window
  28.8 4.3 scatter_custom_fusion
  33.1 6.9 %gather_fusion = bf16[1088]{0:T(1024)(128)(2,1)S(1)} fusion(bf16[1024]{0:T(1024)(128)(2,1)S(1)} %reshape.129, s32[2048]{0:T(1024)S(1)} %get-tuple-element.28), kind=kCustom, calls=%fused_computation | custom fusion | bytes 8704 | tf_op jit(solution)/shard_map/gather | solution.py:50
  40.2 4.9 %gather_fusion.2 = bf16[1088,1024]{1,0:T(8,128)(2,1)} fusion(bf16[128,1024]{1,0:T(8,128)(2,1)S(1)} %copy-done.2, s32[2048]{0:T(1024)S(1)} %get-tuple-element.27), kind=kCustom, calls=%fused_computation.2 | custom fusion | bytes 4460800 | tf_op jit(solution)/shard_map/gather | solution.py:55
  45.2 4.4 gather.25
  49.5 4.9 %gather_fusion.1 = bf16[1088,1024]{1,0:T(8,128)(2,1)} fusion(bf16[128,1024]{1,0:T(8,128)(2,1)S(1)} %copy-done.3, s32[2048]{0:T(1024)S(1)} %get-tuple-element.27), kind=kCustom, calls=%fused_computation.1 | custom fusion | bytes 4460800 | tf_op jit(solution)/shard_map/gather | solution.py:55
  54.4 4.4 gather.23
  58.8 4.3 broadcast_select_fusion
  63.1 86.3 %all_to_all.31 = bf16[64,17,1024]{2,1,0:T(8,128)(2,1)} all-to-all(bf16[64,17,1024]{2,1,0:T(8,128)(2,1)S(1)} %get-tuple-element.23), channel_id=1, replica_groups=mesh['dp'=4,'expert'=64] {'expert'}, dimensions={0} | all-to-all | bytes 4456448 | tf_op jit(solution)/shard_map/all_to_all | solution.py:59
  149.4 6.4 %all-to-all-start.1 = ((bf16[64,17,1024]{2,1,0:T(8,128)(2,1)}), bf16[64,17,1024]{2,1,0:T(8,128)(2,1)}, u32[]{:S(2)}, u32[]{:S(2)}) async-start(bf16[64,17,1024]{2,1,0:T(8,128)(2,1)} %get-tuple-element.24), calls=%async_computation.1 | async-start | bytes 6291456 | tf_op jit(solution)/shard_map/all_to_all | solution.py:60
  155.9 4.3 reshape.131
  160.2 5.0 %convolution_convert_fusion = bf16[1088,768]{1,0:T(8,128)(2,1)} fusion(bf16[1088,1024]{1,0:T(8,128)(2,1)} %reshape.131, bf16[1,768,1024]{2,1,0:T(8,128)(2,1)S(1)} %copy-done), kind=kOutput, calls=%fused_computation.17 | convolution fusion | flops 1712111616 | bytes 5472256 | tf_op jit(solution)/shard_map/dot_general | solution.py:8
  165.2 3.1 convolution_convert_fusion.1
  168.3 60.9 %all-to-all-done.1 = bf16[64,17,1024]{2,1,0:T(8,128)(2,1)} async-done(((bf16[64,17,1024]{2,1,0:T(8,128)(2,1)}), bf16[64,17,1024]{2,1,0:T(8,128)(2,1)}, u32[]{:S(2)}, u32[]{:S(2)}) %all-to-all-start.1) | async-done | bytes 2228256 | tf_op jit(solution)/shard_map/all_to_all | solution.py:60
  229.2 4.4 reshape.130
  233.6 5.2 %convolution_convert_fusion.2 = bf16[1088,768]{1,0:T(8,128)(2,1)} fusion(bf16[1088,1024]{1,0:T(8,128)(2,1)} %reshape.130, bf16[1,768,1024]{2,1,0:T(8,128)(2,1)} %param.13), kind=kOutput, calls=%fused_computation.19 | convolution fusion | flops 1712111616 | bytes 5472256 | tf_op jit(solution)/shard_map/dot_general | solution.py:8
  239.0 15.0 %all_to_all.32 = bf16[64,1,17]{2,1,0:T(2,128)(2,1)S(1)} all-to-all(bf16[64,1,17]{2,1,0:T(2,128)(2,1)S(1)} %all_to_all.25), channel_id=1, replica_groups=mesh['dp'=4,'expert'=64] {'expert'}, dimensions={0} | all-to-all | bytes 4352 | tf_op jit(solution)/shard_map/all_to_all | solution.py:61
  254.3 92.4 %all-reduce.3.cloned.1.call-done = (bf16[1088,768]{1,0:T(8,128)(2,1)}, bf16[1088,768]{1,0:T(8,128)(2,1)}, bf16[1088,768]{1,0:T(8,128)(2,1)}) async-done(((bf16[1088,768]{1,0:T(8,128)(2,1)}, bf16[1088,768]{1,0:T(8,128)(2,1)}, bf16[1088,768]{1,0:T(8,128)(2,1)}), (bf16[1088,768]{1,0:T(8,128)(2,1)}, bf16[1088,768]{1,0:T(8,128)(2,1)}, bf16[1088,768]{1,0:T(8,128)(2,1)})) %all-reduce.3.cloned.1.call-update) | async-done | bytes 5013520 | tf_op jit(solution)/shard_map/psum | solution.py:75
  346.7 5.9 %fusion.3 = (bf16[1088]{0:T(1024)(128)(2,1)S(1)}, bf16[1088,768]{1,0:T(8,128)(2,1)}, bf16[1088,768]{1,0:T(8,128)(2,1)}) fusion(bf16[1088,768]{1,0:T(8,128)(2,1)} %get-tuple-element.15, bf16[1088,768]{1,0:T(8,128)(2,1)} %get-tuple-element.16, bf16[1088,768]{1,0:T(8,128)(2,1)} %get-tuple-element.17, f32[1088]{0:T(1024)S(1)} %reshape.135), kind=kLoop, calls=%fused_computation.21 | loop fusion | flops 16710592 | bytes 8362368 | tf_op jit(solution)/shard_map/reduce_sum | solution.py:23
  353.3 10.8 %all-to-all-start.4 = ((bf16[64,1,17]{2,1,0:T(2,128)(2,1)}), bf16[64,1,17]{2,1,0:T(2,128)(2,1)S(1)}, u32[]{:S(2)}, u32[]{:S(2)}) async-start(bf16[64,1,17]{2,1,0:T(2,128)(2,1)} %convert_element_type.112), calls=%async_computation.4 | async-start | bytes 65536 | tf_op jit(solution)/shard_map/all_to_all | solution.py:94
  364.2 3.5 fusion.15
  367.7 3.8 fusion.1
  371.5 4.3 reshape.132
  375.8 10.5 %all-to-all-start.3 = ((bf16[64,17,1024]{2,1,0:T(8,128)(2,1)}), bf16[64,17,1024]{2,1,0:T(8,128)(2,1)}, u32[]{:S(2)}, u32[]{:S(2)}) async-start(bf16[64,17,1024]{2,1,0:T(8,128)(2,1)} %reshape.132), calls=%async_computation.3 | async-start | bytes 6291456 | tf_op jit(solution)/shard_map/all_to_all | solution.py:87
  386.4 5.7 %fusion.21 = bf16[1,768,1024]{2,1,0:T(8,128)(2,1)} fusion(bf16[1088,768]{1,0:T(8,128)(2,1)} %get-tuple-element.22, bf16[1088,1024]{1,0:T(8,128)(2,1)} %reshape.131), kind=kOutput, calls=%fused_computation.44 | convolution fusion | flops 1712062464 | bytes 5472256 | tf_op jit(solution)/shard_map/dot_general | solution.py:14
  392.0 3.5 fusion.23
  395.5 3.8 fusion.22
  399.6 6.8 %gather_fusion.4 = bf16[1024]{0:T(1024)(128)(2,1)S(1)} fusion(bf16[1088]{0:T(1024)(128)(2,1)S(1)} %reshape.134, s32[1024]{0:T(1024)S(1)} %broadcast_clamp_fusion), kind=kCustom, calls=%fused_computation.4 | custom fusion | bytes 8192 | tf_op jit(solution)/shard_map/gather | solution.py:105
  407.2 52.5 %all-to-all-done.3 = bf16[64,17,1024]{2,1,0:T(8,128)(2,1)} async-done(((bf16[64,17,1024]{2,1,0:T(8,128)(2,1)}), bf16[64,17,1024]{2,1,0:T(8,128)(2,1)}, u32[]{:S(2)}, u32[]{:S(2)}) %all-to-all-start.3) | async-done | bytes 2228256 | tf_op jit(solution)/shard_map/all_to_all | solution.py:87
  459.7 4.3 reshape.133
  464.1 8.1 %gather_fusion.3 = bf16[1024,1024]{1,0:T(8,128)(2,1)} fusion(bf16[1088,1024]{1,0:T(8,128)(2,1)} %reshape.133, s32[1024]{0:T(1024)S(1)} %broadcast_clamp_fusion), kind=kCustom, calls=%fused_computation.3 | custom fusion | bytes 4198400 | tf_op jit(solution)/shard_map/gather | solution.py:102
  472.1 3.7 bitcast_reduce_fusion
  (61 shorter events, 5.9 us)
Async XLA Ops:
  7.2 153.0 %copy-start = (bf16[1,768,1024]{2,1,0:T(8,128)(2,1)S(1)}, bf16[1,768,1024]{2,1,0:T(8,128)(2,1)}, u32[]{:S(2)}) copy-start(bf16[1,768,1024]{2,1,0:T(8,128)(2,1)} %param.11) | copy-start | bytes 4718596
  28.7 11.5 %copy-start.2 = (bf16[128,1024]{1,0:T(8,128)(2,1)S(1)}, bf16[128,1024]{1,0:T(8,128)(2,1)}, u32[]{:S(2)}) copy-start(bf16[128,1024]{1,0:T(8,128)(2,1)} %param.7) | copy-start | bytes 786436
  45.2 4.4 copy-start.3
  149.4 79.8 %all-to-all-start.1 = ((bf16[64,17,1024]{2,1,0:T(8,128)(2,1)}), bf16[64,17,1024]{2,1,0:T(8,128)(2,1)}, u32[]{:S(2)}, u32[]{:S(2)}) async-start(bf16[64,17,1024]{2,1,0:T(8,128)(2,1)} %get-tuple-element.24), calls=%async_computation.1 | async-start | bytes 6291456 | tf_op jit(solution)/shard_map/all_to_all | solution.py:60
  155.8 190.9 %all-reduce.3.cloned.1.call-start = ((), (), s32[]{:S(2)}) async-start(), calls=%async_computation.5 | async-start | bytes 10027008 | tf_op jit(solution)/shard_map/psum | solution.py:75
  160.2 5.0 %copy-start.4 = (bf16[1088,1024]{1,0:T(8,128)(2,1)S(1)}, bf16[1088,1024]{1,0:T(8,128)(2,1)}, u32[]{:S(2)}) copy-start(bf16[1088,1024]{1,0:T(8,128)(2,1)} %reshape.131) | copy-start | bytes 6684676
  160.2 5.0 %copy-start.11 = (bf16[1,768,1024]{2,1,0:T(8,128)(2,1)S(1)}, bf16[1,768,1024]{2,1,0:T(8,128)(2,1)}, u32[]{:S(2)}) copy-start(bf16[1,768,1024]{2,1,0:T(8,128)(2,1)} %param.12) | copy-start | bytes 4718596
  353.3 22.5 %all-to-all-start.4 = ((bf16[64,1,17]{2,1,0:T(2,128)(2,1)}), bf16[64,1,17]{2,1,0:T(2,128)(2,1)S(1)}, u32[]{:S(2)}, u32[]{:S(2)}) async-start(bf16[64,1,17]{2,1,0:T(2,128)(2,1)} %convert_element_type.112), calls=%async_computation.4 | async-start | bytes 65536 | tf_op jit(solution)/shard_map/all_to_all | solution.py:94
  364.2 3.5 copy-start.7
  364.2 3.5 copy-start.8
  364.2 3.5 copy-start.12
  375.8 83.9 %all-to-all-start.3 = ((bf16[64,17,1024]{2,1,0:T(8,128)(2,1)}), bf16[64,17,1024]{2,1,0:T(8,128)(2,1)}, u32[]{:S(2)}, u32[]{:S(2)}) async-start(bf16[64,17,1024]{2,1,0:T(8,128)(2,1)} %reshape.132), calls=%async_computation.3 | async-start | bytes 6291456 | tf_op jit(solution)/shard_map/all_to_all | solution.py:87
  386.3 5.7 %copy-start.6 = (bf16[1088,1024]{1,0:T(8,128)(2,1)S(1)}, bf16[1088,1024]{1,0:T(8,128)(2,1)}, u32[]{:S(2)}) copy-start(bf16[1088,1024]{1,0:T(8,128)(2,1)} %reshape.130) | copy-start | bytes 6684676
  386.4 5.7 %copy-start.10 = (bf16[1088,768]{1,0:T(8,128)(2,1)S(1)}, bf16[1088,768]{1,0:T(8,128)(2,1)}, u32[]{:S(2)}) copy-start(bf16[1088,768]{1,0:T(8,128)(2,1)} %get-tuple-element.19) | copy-start | bytes 5013508
  392.0 3.5 copy-start.5
  392.0 3.5 copy-start.9
  464.1 11.8 %copy-start.1 = (bf16[1,768,1024]{2,1,0:T(8,128)(2,1)S(1)}, bf16[1,768,1024]{2,1,0:T(8,128)(2,1)}, u32[]{:S(2)}) copy-start(bf16[1,768,1024]{2,1,0:T(8,128)(2,1)} %param.11) | copy-start | bytes 4718596
Sparse Core Ops, SparseCore 0:
  238.9 107.7 all-reduce.2
where the time goes:
time: 484 us; the launch traced here: 483 us
  waiting for transfers between devices  206 us (43%)
  blocking collectives  101 us (21%)
  local copies, waits for them, and re-layouts  66.7 us (14%)
  matrix products  33.6 us (7%)
  other arithmetic  33.1 us (7%)
  starting transfers between devices  27.7 us (6%)
  between operations  14.3 us (3%)
    psum x1, waiting for transfers between devices, local(): lax.psum(back_part.astype(jnp.bfloat16), 'dp').astype(jnp.float32)  92.4 us
    all_to_all x1, blocking collectives, local(): lax.all_to_all(pack_rows(tokens), 'expert', split_axis=0, concat_axis=0,...  86.3 us
    all_to_all x1, waiting for transfers between devices, local(): lax.all_to_all(pack_rows(cotangent), 'expert', split_axis=0, concat_axis=...  60.9 us
    all_to_all x1, waiting for transfers between devices, local(): lax.all_to_all(row_term.reshape(experts, slot_count, features), 'expert',...  52.5 us
    gather x4, local copies, waits for them, and re-layouts, pack_rows(): source[owners]  18.6 us
    another operation x3, other arithmetic  18.2 us
    all_to_all x1, blocking collectives, local(): lax.all_to_all(send_probs, 'expert', split_axis=0, concat_axis=0, tiled=T...  15 us
    dot_general x3, matrix products, contract_last(): lax.dot_general(left_matrix, right_matrix, (((1,), (1,)), ((), ())), pref...  13.3 us
  transfers between devices with their start and end apart: 4, of which 3 were waited for; matrix products, arithmetic and copies ran while one was open for 9% of the time, Pallas kernels for 0%

commit v1 on v0

v1 whole, which is shorter than its diff:
```python
import functools
import types

import jax
import jax.numpy as jnp
from jax import lax
from jax.experimental import pallas as pl
from jax.experimental.pallas import tpu as pltpu
from jax.sharding import PartitionSpec as P

MESH = pl.DeviceIdType.MESH
LANES = 128
MAIN = 16
SPARE = 8
F32 = jnp.float32
BF16 = jnp.bfloat16


def dot(left, right, left_dim, right_dim):
    return lax.dot_general(
        left, right, (((left_dim,), (right_dim,)), ((), ())), preferred_element_type=F32
    )


def make_layout(n_x, n_z, n_core, rounds):
    order = [k for ks, _ in rounds for k in ks]
    return types.SimpleNamespace(
        n_x=n_x,
        n_z=n_z,
        n_core=n_core,
        peers=n_x * n_core,
        rounds=rounds,
        place={k: i for i, k in enumerate(order)},
        order=order,
    )


def kernel(lay, steps, tok, cot, aux, wg, wu, wd, tg_out, pg_out, gg_out, ug_out, dg_out, *scratch):
    (
        tok_all, cot_all, aux_all, hot, hot_spare, hot_spare_p, sent, sent_spare, rows, rows_spare,
        weights, part, part_spare, first, first_spare, second, second_spare, acts, acts_spare,
        term, term_spare, back, back_spare, z_sent, z_right, z_left, pg_sent, pg_got, grads,
        w_sem, own_sem, out_sem, aux_ss, aux_rs, ag_ss, ag_rs, d_ss, d_rs, y_ss, y_rs, yo_ss, yo_rs,
        t_ss, t_rs, z_ss, z_rs, pg_ss, pg_rs,
    ) = scratch
    n_z, peers, n_core = lay.n_z, lay.peers, lay.n_core
    n_tok, feats = tok.shape
    units = wg.shape[0]
    row_w = 2 * feats + LANES
    act_w = 3 * units + LANES
    term_w = feats + LANES
    half = 3 * units // 2
    act_half = ((act_w // LANES + 1) // 2) * LANES
    per = peers // 4
    far = n_z // 2
    y = lax.axis_index("dp")
    e = lax.axis_index("expert")
    x, z, core = e // (n_z * n_core), (e // n_core) % n_z, e % n_core
    me = x * n_core + core

    def place_of(peer, plane):
        return ((peer // n_core) * n_z + plane) * n_core + peer % n_core

    z_next = (y, place_of(me, (z + 1) % n_z))
    z_prev = (y, place_of(me, (z + n_z - 1) % n_z))
    y_next = ((y + 1) % 4, e)
    y_prev = ((y + 3) % 4, e)
    right_y, left_y, across_y = (y + 1) % 4, (y + 3) % 4, (y + 2) % 4

    def remote(src, dst, send_sem, recv_sem, device):
        return pltpu.make_async_remote_copy(
            src_ref=src, dst_ref=dst, send_sem=send_sem, recv_sem=recv_sem,
            device_id=device, device_id_type=MESH,
        )

    pending = []

    def go(copy):
        copy.start()
        pending.append(copy)
        return copy

    loads = [
        pltpu.make_async_copy(w, weights.at[pl.ds(i * units, units)], w_sem.at[i])
        for i, w in enumerate((wg, wu, wd))
    ]
    own = [
        pltpu.make_async_copy(tok, tok_all.at[0], own_sem.at[0]),
        pltpu.make_async_copy(cot, cot_all.at[0], own_sem.at[1]),
        pltpu.make_async_copy(aux, aux_all.at[0], own_sem.at[2]),
    ]
    for copy in own + loads:
        copy.start()

    barrier = pltpu.get_barrier_semaphore()
    for device in (y_next, y_prev):
        pl.semaphore_signal(barrier, inc=1, device_id=device, device_id_type=MESH)
    for k in range(1, n_z):
        pl.semaphore_signal(
            barrier, inc=1, device_id=(y, place_of(me, (z + k) % n_z)), device_id_type=MESH
        )
    for k in range(1, peers):
        pl.semaphore_signal(
            barrier, inc=1, device_id=(y, place_of((me + k) % peers, z)), device_id_type=MESH
        )
    pl.semaphore_wait(barrier, 2 + n_z - 1 + peers - 1)

    def z_span(hop, way):
        if hop < far:
            return pl.ds(0, n_tok)
        return pl.ds(0 if way == 0 else n_tok // 2, n_tok // 2)

    def z_hop(hop, way):
        sign = -1 if way == 0 else 1
        src_slot, dst_slot = (sign * (hop - 1)) % n_z, (sign * hop) % n_z
        span = z_span(hop, way)
        out = []
        for i, (mine, held) in enumerate(((tok, tok_all), (cot, cot_all))):
            src = mine.at[span] if hop == 1 else held.at[src_slot, span]
            out.append(
                remote(
                    src, held.at[dst_slot, span], ag_ss.at[way, hop - 1, i],
                    ag_rs.at[way, hop - 1, i], z_next if way == 0 else z_prev,
                )
            )
        return out

    arrived = {}

    def z_send(hop):
        for way in (0, 1):
            arrived[hop, way] = [go(copy) for copy in z_hop(hop, way)]

    def z_wait(hop, ways=(0, 1)):
        for way in ways:
            for copy in arrived[hop, way]:
                copy.wait_recv()

    aux_copies = {}

    def aux_send():
        for k in range(1, n_z):
            aux_copies[k] = go(
                remote(
                    aux, aux_all.at[k], aux_ss.at[k], aux_rs.at[k],
                    (y, place_of(me, (z + n_z - k) % n_z)),
                )
            )

    names = [place_of(j, z) for j in range(peers)]

    def read_table(slot):
        table = aux_all[slot]
        ids = table[0:8].astype(jnp.int32)
        return ids, table[8:16]

    def pick(pos, slot):
        ids, probs = read_table(slot)
        hits = jnp.concatenate(
            [jnp.sum(jnp.where(ids == n, 1.0, 0.0), axis=0, keepdims=True) for n in names], axis=0
        )
        given = [jnp.sum(jnp.where(ids == n, probs, 0.0), axis=0, keepdims=True) for n in names]
        before = (
            lax.broadcasted_iota(jnp.int32, (n_tok, n_tok), 0)
            < lax.broadcasted_iota(jnp.int32, (n_tok, n_tok), 1)
        )
        if peers % 8:
            hits_full = jnp.concatenate([hits, jnp.zeros((8 - peers, n_tok), F32)], axis=0)
        else:
            hits_full = hits
        rank = dot(hits_full.astype(BF16), jnp.where(before, 1.0, 0.0).astype(BF16), 1, 0)
        rank = jnp.where(hits > 0.5, rank[0:peers], -1.0)
        s_main = lax.broadcasted_iota(jnp.int32, (MAIN, n_tok), 0).astype(F32)
        s_spare = lax.broadcasted_iota(jnp.int32, (SPARE, n_tok), 0)
        main, main_p, spare, spare_p = [], [], [], []
        for j in range(peers):
            r = rank[j : j + 1]
            one = jnp.where(jnp.broadcast_to(r, (MAIN, n_tok)) == s_main, 1.0, 0.0)
            main.append(one)
            main_p.append(one * jnp.broadcast_to(given[j], (MAIN, n_tok)))
            over = jnp.where(r > MAIN - 0.5, 1.0, 0.0)
            sp = jnp.where(s_spare == slot, jnp.broadcast_to(over, (SPARE, n_tok)), 0.0)
            spare.append(sp)
            spare_p.append(sp * jnp.broadcast_to(given[j], (SPARE, n_tok)))
        one = jnp.concatenate(main, axis=0).astype(BF16)
        hot[pos] = one
        cols = pl.ds(slot * n_tok, n_tok)
        hot_spare[:, cols] = jnp.concatenate(spare, axis=0).astype(BF16)
        hot_spare_p[:, cols] = jnp.concatenate(spare_p, axis=0).astype(BF16)
        ones = jnp.ones((n_tok, LANES), BF16)
        shape = (peers, MAIN, -1)
        probs_rows = dot(jnp.concatenate(main_p, axis=0).astype(BF16), ones, 1, 0)
        sent[pos, :, :, 2 * feats :] = probs_rows.astype(BF16).reshape(peers, MAIN, LANES)
        sent[pos, :, :, 0:feats] = dot(one, tok_all[slot], 1, 0).astype(BF16).reshape(peers, MAIN, feats)
        sent[pos, :, :, feats : 2 * feats] = (
            dot(one, cot_all[slot], 1, 0).astype(BF16).reshape(peers, MAIN, feats)
        )

    def exchange(src, dst, send_sems, recv_sems, row):
        def copy_to(i):
            j = (me + i) % peers
            return remote(
                src.at[j], dst.at[me], send_sems.at[row, i], recv_sems.at[row, me],
                (y, place_of(j, z)),
            )

        def copy_from(i):
            j = (me + i) % peers
            return remote(
                src.at[j], dst.at[j], send_sems.at[row, i], recv_sems.at[row, j],
                (y, place_of(j, z)),
            )

        def start():
            @pl.loop(1, peers)
            def _(i):
                copy_to(i).start()

            dst[pl.ds(me, 1)] = src[pl.ds(me, 1)]

        def wait():
            @pl.loop(1, peers)
            def _(i):
                copy_from(i).wait_recv()

        def finish():
            @pl.loop(1, peers)
            def _(i):
                copy_to(i).wait_send()

        return types.SimpleNamespace(start=start, wait=wait, finish=finish)

    n_pos = len(lay.order)
    dispatch = {
        k: exchange(sent.at[p], rows.at[p], d_ss, d_rs, p) for k, p in lay.place.items()
    }
    dispatch_spare = exchange(sent_spare, rows_spare, d_ss, d_rs, n_pos)
    ret = {k: exchange(term.at[p], back.at[p], t_ss, t_rs, p) for k, p in lay.place.items()}
    ret_spare = exchange(term_spare, back_spare, t_ss, t_rs, n_pos)

    def gather(k):
        if k:
            aux_copies[k % n_z].wait_recv()
        pick(lay.place[k], k % n_z)
        dispatch[k].start()

    def gather_spare():
        ones = jnp.ones((n_z * n_tok, LANES), BF16)
        shape = (peers, SPARE)
        sent_spare[:, :, 2 * feats :] = (
            dot(hot_spare_p[...], ones, 1, 0).astype(BF16).reshape(shape + (LANES,))
        )
        for i, held in enumerate((tok_all, cot_all)):
            block = held[...].reshape(n_z * n_tok, feats)
            sent_spare[:, :, i * feats : (i + 1) * feats] = (
                dot(hot_spare[...], block, 1, 0).astype(BF16).reshape(shape + (feats,))
            )
        dispatch_spare.start()

    tile = min(256, units)

    def segment(r):
        ks, spare = lay.rounds[r]
        first_pos = lay.place[ks[0]]
        return pl.ds(first_pos, len(ks)), len(ks), spare

    y_copies = {}

    def y_send(kind, r, way, src, dst, src_spare, dst_spare, spare):
        device = y_next if way == 0 else y_prev
        made = [go(remote(src, dst, y_ss.at[kind, r, way], y_rs.at[kind, r, way], device))]
        if spare:
            made.append(
                go(remote(src_spare, dst_spare, yo_ss.at[kind, way], yo_rs.at[kind, way], device))
            )
        y_copies[kind, r, way] = made

    def y_wait(kind, r, way):
        for copy in y_copies[kind, r, way]:
            copy.wait_recv()

    def shard(index):
        return pl.ds(index * per, per)

    def project(r):
        span, n, spare = segment(r)
        for k in lay.rounds[r][0]:
            dispatch[k].wait()
        if spare:
            dispatch_spare.wait()
        if r == 0:
            for copy in loads:
                copy.wait()
        for base, count, col in ((0, 2 * units // tile, 0), (2 * units, units // tile, feats)):
            @pl.loop(0, count)
            def _(i):
                at = pl.multiple_of(base + i * tile, tile)
                block = weights[pl.ds(at, tile)]
                left = rows[span, :, :, col : col + feats].reshape(n * peers * MAIN, feats)
                out = dot(left, block, 1, 1).astype(BF16)
                part[span, :, :, pl.ds(at, tile)] = out.reshape(n, peers, MAIN, tile)
                if spare:
                    left = rows_spare[:, :, col : col + feats].reshape(peers * SPARE, feats)
                    out = dot(left, block, 1, 1).astype(BF16)
                    part_spare[:, :, pl.ds(at, tile)] = out.reshape(4, peers * SPARE // 4, tile)
        for way, cols in ((0, pl.ds(0, half)), (1, pl.ds(half, half))):
            y_send(
                0, r, way, part.at[span, shard(across_y), :, cols], first.at[way, span],
                part_spare.at[across_y, :, cols], first_spare.at[way], spare,
            )

    def fold(r):
        span, n, spare = segment(r)
        for way, cols, owner in ((0, pl.ds(0, half), right_y), (1, pl.ds(half, half), left_y)):
            y_wait(0, r, way)
            part[span, shard(owner), :, cols] = (
                part[span, shard(owner), :, cols].astype(F32) + first[way, span].astype(F32)
            ).astype(BF16)
            if spare:
                part_spare[pl.ds(owner, 1), :, cols] = (
                    part_spare[pl.ds(owner, 1), :, cols].astype(F32)
                    + first_spare[pl.ds(way, 1)].astype(F32)
                ).astype(BF16)
            y_send(
                1, r, way, part.at[span, shard(owner)], second.at[way, span],
                part_spare.at[owner], second_spare.at[way], spare,
            )

    def act_math(values, probs, units_w):
        gate, up, bck = values
        s = jax.nn.sigmoid(gate)
        silu = gate * s
        hidden = (silu * up).astype(BF16)
        pv = jnp.sum(hidden.astype(F32) * bck, axis=1, keepdims=True)
        p = jnp.concatenate([probs.astype(F32)] * (units_w // LANES), axis=1)
        gb = p * bck
        d_gate = (gb * up * s * (1.0 + gate * (1.0 - s))).astype(BF16)
        d_up = (gb * silu).astype(BF16)
        return hidden, d_gate, d_up, jnp.broadcast_to(pv, (pv.shape[0], LANES)).astype(BF16)

    def activate(r):
        span, n, spare = segment(r)
        y_wait(1, r, 0)
        y_wait(1, r, 1)
        count = n * per * MAIN

        def value(i):
            cols = pl.ds(i * units, units)
            return (
                part[span, shard(y), :, cols].astype(F32)
                + second[0, span, :, :, cols].astype(F32)
                + second[1, span, :, :, cols].astype(F32)
            ).reshape(count, units)

        probs = rows[span, shard(y), :, 2 * feats :].reshape(count, LANES)
        hidden, d_gate, d_up, pv = act_math([value(i) for i in range(3)], probs, units)
        for i, v in enumerate((hidden, d_gate, d_up)):
            acts[span, shard(y), :, i * units : (i + 1) * units] = v.reshape(n, per, MAIN, units)
        acts[span, shard(y), :, 3 * units :] = pv.reshape(n, per, MAIN, LANES)
        if spare:
            count = per * SPARE

            def value_spare(i):
                cols = pl.ds(i * units, units)
                return (
                    part_spare[pl.ds(y, 1), :, cols].astype(F32)
                    + second_spare[pl.ds(0, 1), :, cols].astype(F32)
                    + second_spare[pl.ds(1, 1), :, cols].astype(F32)
                ).reshape(count, units)

            probs = rows_spare[shard(y), :, 2 * feats :].reshape(count, LANES)
            hidden, d_gate, d_up, pv = act_math([value_spare(i) for i in range(3)], probs, units)
            for i, v in enumerate((hidden, d_gate, d_up)):
                acts_spare[pl.ds(y, 1), :, i * units : (i + 1) * units] = v.reshape(1, count, units)
            acts_spare[pl.ds(y, 1), :, 3 * units :] = pv.reshape(1, count, LANES)
        for way in (0, 1):
            y_send(
                2, r, way, acts.at[span, shard(y)], acts.at[span, shard(y)],
                acts_spare.at[y], acts_spare.at[y], spare,
            )

    def relay(r):
        span, n, spare = segment(r)
        for way, cols, owner in (
            (0, pl.ds(0, act_half), left_y), (1, pl.ds(act_half, act_w - act_half), right_y)
        ):
            y_wait(2, r, way)
            y_send(
                3, r, way, acts.at[span, shard(owner), :, cols], acts.at[span, shard(owner), :, cols],
                acts_spare.at[owner, :, cols], acts_spare.at[owner, :, cols], spare,
            )

    f_tile = min(256, feats)

    def send_back(r):
        span, n, spare = segment(r)
        y_wait(3, r, 0)
        y_wait(3, r, 1)

        @pl.loop(0, feats // f_tile)
        def _(i):
            at = pl.multiple_of(i * f_tile, f_tile)
            block = weights[0 : 2 * units, pl.ds(at, f_tile)]
            left = acts[span, :, :, units : 3 * units].reshape(n * peers * MAIN, 2 * units)
            term[span, :, :, pl.ds(at, f_tile)] = (
                dot(left, block, 1, 0).astype(BF16).reshape(n, peers, MAIN, f_tile)
            )
            if spare:
                left = acts_spare[:, :, units : 3 * units].reshape(peers * SPARE, 2 * units)
                term_spare[:, :, pl.ds(at, f_tile)] = (
                    dot(left, block, 1, 0).astype(BF16).reshape(peers, SPARE, f_tile)
                )

        term[span, :, :, feats:] = acts[span, :, :, 3 * units :]
        for k in lay.rounds[r][0]:
            ret[k].start()
        if spare:
            term_spare[:, :, feats:] = acts_spare[:, :, 3 * units :].reshape(peers, SPARE, LANES)
            ret_spare.start()

    z_copies = {}
    pg_copies = {}

    def wait_spare():
        ret_spare.wait()

    def combine(k):
        pos, slot = lay.place[k], k % n_z
        ret[k].wait()
        got = back[pos].reshape(peers * MAIN, term_w)
        got_spare = back_spare[...].reshape(peers * SPARE, term_w)
        one = hot[pos]
        spare = hot_spare[:, pl.ds(slot * n_tok, n_tok)]
        total = dot(one, got[:, 0:feats], 0, 0) + dot(spare, got_spare[:, 0:feats], 0, 0)
        ids, _ = read_table(slot)
        weighted = one.astype(F32) * got[:, feats:].astype(F32)
        weighted_spare = spare.astype(F32) * got_spare[:, feats:].astype(F32)
        grad = jnp.zeros((8, n_tok), F32)
        for j in range(peers):
            v = jnp.sum(weighted[j * MAIN : (j + 1) * MAIN], axis=0, keepdims=True)
            v = v + jnp.sum(weighted_spare[j * SPARE : (j + 1) * SPARE], axis=0, keepdims=True)
            grad = grad + jnp.where(ids == names[j], jnp.broadcast_to(v, (8, n_tok)), 0.0)
        if k == 0:
            pg_got[0] = grad
        else:
            pg_sent[slot] = grad
            pg_copies[slot] = go(
                remote(
                    pg_sent.at[slot], pg_got.at[n_z - slot], pg_ss.at[slot], pg_rs.at[n_z - slot],
                    (y, place_of(me, (z + slot) % n_z)),
                )
            )
        k_signed = k if k <= far else k - n_z
        if k_signed == far:
            z_sent[slot] = total.astype(BF16)
            lo, hi = pl.ds(0, n_tok // 2), pl.ds(n_tok // 2, n_tok // 2)
            z_copies[0, far] = go(
                remote(z_sent.at[slot, lo], z_right.at[far - 1, lo], z_ss.at[0, far],
                       z_rs.at[0, far - 1], z_next)
            )
            z_copies[1, far] = go(
                remote(z_sent.at[slot, hi], z_left.at[far - 1, hi], z_ss.at[1, far],
                       z_rs.at[1, far - 1], z_prev)
            )
            return
        h = n_tok // 2
        if k_signed != 0:
            way = 0 if k_signed > 0 else 1
            dist = abs(k_signed)
            z_copies[way, dist + 1].wait_recv()
            held = z_right if way == 0 else z_left
            if dist == far - 1:
                if way == 0:
                    z_sent[slot, 0:h] = (total[0:h] + held[dist, 0:h].astype(F32)).astype(BF16)
                    z_sent[slot, h:] = total[h:].astype(BF16)
                else:
                    z_sent[slot, h:] = (total[h:] + held[dist, h:].astype(F32)).astype(BF16)
                    z_sent[slot, 0:h] = total[0:h].astype(BF16)
            else:
                z_sent[slot] = (total + held[dist].astype(F32)).astype(BF16)
            z_copies[way, dist] = go(
                remote(z_sent.at[slot], held.at[dist - 1], z_ss.at[way, dist],
                       z_rs.at[way, dist - 1], z_next if way == 0 else z_prev)
            )
            return
        z_copies[0, 1].wait_recv()
        z_copies[1, 1].wait_recv()
        tg_out[...] = (total + z_right[0].astype(F32) + z_left[0].astype(F32)).astype(BF16)

    def finish_probs():
        for slot in pg_copies:
            pg_copies[slot].wait_recv()
        total = pg_got[0]
        for slot in range(1, n_z):
            total = total + pg_got[slot]
        pg_out[...] = total

    outs = [
        pltpu.make_async_copy(grads.at[pl.ds(i * units, units)], o, out_sem.at[i])
        for i, o in enumerate((gg_out, ug_out, dg_out))
    ]

    all_rows = n_pos * peers * MAIN

    def grads_in():
        left_full = rows[:, :, :, 0:feats].reshape(all_rows, feats)
        left_spare = rows_spare[:, :, 0:feats].reshape(peers * SPARE, feats)

        @pl.loop(0, 2 * units // tile)
        def _(i):
            at = pl.multiple_of(units + i * tile, tile)
            a = acts[:, :, :, pl.ds(at, tile)].reshape(all_rows, tile)
            b = acts_spare[:, :, pl.ds(at, tile)].reshape(peers * SPARE, tile)
            full = rows[:, :, :, 0:feats].reshape(all_rows, feats)
            spare = rows_spare[:, :, 0:feats].reshape(peers * SPARE, feats)
            grads[pl.ds(pl.multiple_of(i * tile, tile), tile)] = (
                dot(a, full, 0, 0) + dot(b, spare, 0, 0)
            ).astype(BF16)

        outs[0].start()
        outs[1].start()

    def scale():
        @pl.loop(0, n_pos)
        def _(i):
            p = rows[pl.ds(i, 1), :, :, 2 * feats :].astype(F32)
            p = jnp.concatenate([p] * (feats // LANES), axis=3)
            c = rows[pl.ds(i, 1), :, :, feats : 2 * feats].astype(F32)
            rows[pl.ds(i, 1), :, :, feats : 2 * feats] = (p * c).astype(BF16)

        p = jnp.concatenate([rows_spare[:, :, 2 * feats :].astype(F32)] * (feats // LANES), axis=2)
        c = rows_spare[:, :, feats : 2 * feats].astype(F32)
        rows_spare[:, :, feats : 2 * feats] = (p * c).astype(BF16)

    def grads_down():
        @pl.loop(0, units // tile)
        def _(i):
            at = pl.multiple_of(i * tile, tile)
            a = acts[:, :, :, pl.ds(at, tile)].reshape(all_rows, tile)
            b = acts_spare[:, :, pl.ds(at, tile)].reshape(peers * SPARE, tile)
            full = rows[:, :, :, feats : 2 * feats].reshape(all_rows, feats)
            spare = rows_spare[:, :, feats : 2 * feats].reshape(peers * SPARE, feats)
            grads[pl.ds(pl.multiple_of(2 * units + i * tile, tile), tile)] = (
                dot(a, full, 0, 0) + dot(b, spare, 0, 0)
            ).astype(BF16)

        outs[2].start()

    def own_wait():
        for copy in own:
            copy.wait()

    table = dict(
        aux_send=aux_send, z_send=z_send, z_wait=z_wait, own_wait=own_wait, gather=gather,
        gather_spare=gather_spare, project=project, fold=fold, activate=activate, relay=relay,
        send_back=send_back, wait_spare=wait_spare, combine=combine, finish_probs=finish_probs,
        grads_in=grads_in, scale=scale, grads_down=grads_down,
    )
    for name, *args in steps:
        table[name](*args)
    for copy in outs:
        copy.wait()
    for copy in pending:
        copy.wait_send()
    for group in (dispatch, ret):
        for item in group.values():
            item.finish()
    dispatch_spare.finish()
    ret_spare.finish()


def plan(n_z):
    if n_z == 4:
        rounds = [([0], False), ([2, 1], True), ([-1], False)]
        steps = [
            ("aux_send",), ("z_send", 1), ("own_wait",), ("gather", 0),
            ("z_wait", 1), ("z_send", 2), ("gather", 1), ("gather", -1), ("project", 0), ("fold", 0),
            ("activate", 0), ("z_wait", 2), ("gather", 2), ("gather_spare",), ("relay", 0),
            ("project", 1), ("fold", 1), ("send_back", 0), ("activate", 1), ("project", 2),
            ("relay", 1), ("fold", 2), ("send_back", 1), ("activate", 2), ("wait_spare",),
            ("combine", 2), ("combine", 1), ("relay", 2), ("scale",),
            ("send_back", 2), ("grads_in",), ("combine", -1), ("combine", 0), ("grads_down",),
            ("finish_probs",),
        ]
        return rounds, steps
    rounds = [([0], False), ([1], False), ([2, -2], False), ([3, 4], True), ([-3], False), ([-1], False)]
    steps = [
        ("aux_send",), ("z_send", 1), ("own_wait",), ("gather", 0),
        ("project", 0), ("fold", 0),
        ("z_wait", 1), ("z_send", 2), ("gather", 1), ("gather", -1),
        ("activate", 0), ("relay", 0),
        ("z_wait", 2), ("z_send", 3), ("gather", 2), ("gather", -2),
        ("project", 1), ("send_back", 0), ("fold", 1), ("activate", 1),
        ("z_wait", 3), ("z_send", 4), ("gather", 3), ("gather", -3), ("relay", 1),
        ("project", 2), ("send_back", 1), ("fold", 2),
        ("z_wait", 4), ("gather", 4), ("gather_spare",),
        ("activate", 2), ("project", 3), ("relay", 2), ("fold", 3), ("send_back", 2),
        ("activate", 3), ("project", 4), ("fold", 4), ("relay", 3), ("activate", 4), ("project", 5),
        ("send_back", 3), ("fold", 5), ("relay", 4), ("scale",), ("activate", 5),
        ("wait_spare",), ("combine", 4), ("send_back", 4), ("combine", 3),
        ("relay", 5), ("combine", -3), ("combine", 2), ("combine", -2), ("send_back", 5),
        ("combine", 1), ("grads_in",), ("combine", -1), ("grads_down",), ("combine", 0),
        ("finish_probs",),
    ]
    return rounds, steps


def build(n_x, n_z, n_core):
    rounds, steps = plan(n_z)
    lay = make_layout(n_x, n_z, n_core, rounds)

    def local(tokens, cotangent, router_probs, expert_ids, w_gate, w_up, w_down):
        n_tok, feats = tokens.shape
        units = w_gate.shape[1]
        peers, n_pos, per = lay.peers, n_z, lay.peers // 4
        row_w, act_w, term_w = 2 * feats + LANES, 3 * units + LANES, feats + LANES
        extra = 8 - expert_ids.shape[1]
        aux = jnp.concatenate(
            [
                jnp.pad(expert_ids.T.astype(F32), ((0, extra), (0, 0)), constant_values=-1.0),
                jnp.pad(router_probs.T.astype(F32), ((0, extra), (0, 0))),
            ],
            axis=0,
        )
        half = 3 * units // 2
        spare_rows = peers * SPARE // 4
        dma = pltpu.SemaphoreType.DMA
        n_r = len(rounds)
        vm = pltpu.VMEM
        scratch = [
            vm((n_z, n_tok, feats), BF16), vm((n_z, n_tok, feats), BF16), vm((n_z, 16, n_tok), F32),
            vm((n_pos, peers * MAIN, n_tok), BF16), vm((peers * SPARE, n_z * n_tok), BF16),
            vm((peers * SPARE, n_z * n_tok), BF16),
            vm((n_pos, peers, MAIN, row_w), BF16), vm((peers, SPARE, row_w), BF16),
            vm((n_pos, peers, MAIN, row_w), BF16), vm((peers, SPARE, row_w), BF16),
            vm((3 * units, feats), BF16),
            vm((n_pos, peers, MAIN, 3 * units), BF16), vm((4, spare_rows, 3 * units), BF16),
            vm((2, n_pos, per, MAIN, half), BF16), vm((2, spare_rows, half), BF16),
            vm((2, n_pos, per, MAIN, 3 * units), BF16), vm((2, spare_rows, 3 * units), BF16),
            vm((n_pos, peers, MAIN, act_w), BF16), vm((4, spare_rows, act_w), BF16),
            vm((n_pos, peers, MAIN, term_w), BF16), vm((peers, SPARE, term_w), BF16),
            vm((n_pos, peers, MAIN, term_w), BF16), vm((peers, SPARE, term_w), BF16),
            vm((n_z, n_tok, feats), BF16), vm((n_z // 2, n_tok, feats), BF16),
            vm((n_z // 2, n_tok, feats), BF16),
            vm((n_z, 8, n_tok), F32), vm((n_z, 8, n_tok), F32), vm((3 * units, feats), BF16),
            dma((3,)), dma((3,)), dma((3,)), dma((n_z,)), dma((n_z,)),
            dma((2, n_z // 2, 2)), dma((2, n_z // 2, 2)),
            dma((n_pos + 1, peers)), dma((n_pos + 1, peers)),
            dma((4, n_r, 2)), dma((4, n_r, 2)), dma((4, 2)), dma((4, 2)),
            dma((n_pos + 1, peers)), dma((n_pos + 1, peers)),
            dma((2, n_z // 2 + 1)), dma((2, n_z // 2 + 1)), dma((n_z,)), dma((n_z,)),
        ]
        sds = jax.ShapeDtypeStruct
        anywhere = pl.BlockSpec(memory_space=pl.ANY)
        inside = pl.BlockSpec(memory_space=pltpu.VMEM)
        tg, pg, gg, ug, dg = pl.pallas_call(
            functools.partial(kernel, lay, steps),
            out_shape=(
                sds((n_tok, feats), BF16), sds((8, n_tok), F32), sds((units, feats), BF16),
                sds((units, feats), BF16), sds((units, feats), BF16),
            ),
            in_specs=[anywhere] * 6,
            out_specs=(inside, inside, anywhere, anywhere, anywhere),
            scratch_shapes=scratch,
            compiler_params=pltpu.CompilerParams(
                collective_id=0, has_side_effects=True, vmem_limit_bytes=63 * 1024 * 1024
            ),
        )(tokens, cotangent, aux, w_gate[0], w_up[0], w_down[0])
        return tg, pg[: expert_ids.shape[1]].T, gg[None], ug[None], dg[None]

    return local


def solution(mesh, shape=(4, 8, 2)):
    return jax.shard_map(
        build(*shape),
        mesh=mesh,
        in_specs=(
            P("expert", "dp"), P("expert", "dp"), P("expert", None), P("expert", None),
            P("expert", None, "dp"), P("expert", None, "dp"), P("expert", None, "dp"),
        ),
        out_specs=(
            P("expert", "dp"), P("expert", None),
            P("expert", None, "dp"), P("expert", None, "dp"), P("expert", None, "dp"),
        ),
        check_vma=False,
    )
```

time: 484 us -> 183 us (0.38)
  waiting for transfers between devices: 206 us -> 0 us
  Pallas kernels: 0 us -> 170 us
  blocking collectives: 101 us -> 0 us
  local copies, waits for them, and re-layouts: 66.7 us -> 8.84 us
  matrix products: 33.6 us -> 0 us
  other arithmetic: 33.1 us -> 1.98 us
  starting transfers between devices: 27.7 us -> 0 us
  between operations: 14.3 us -> 0.64 us
    pallas_call x0 -> x1, Pallas kernels: none -> 170 us  [local(): pl.pallas_call(functools.partial(kernel, lay, steps), out_shape=(sds((n_t...]
    all_to_all x3 -> x0, waiting for transfers between devices: 113 us -> none  [the longest x1 60.9 us: local(): lax.all_to_all(pack_rows(cotangent), 'expert', split_axis=0, concat_axis=...]
    all_to_all x2 -> x0, blocking collectives: 101 us -> none  [the longest x1 86.3 us: local(): lax.all_to_all(pack_rows(tokens), 'expert', split_axis=0, concat_axis=0,...]
    psum x1 -> x0, waiting for transfers between devices: 92.4 us -> none  [local(): lax.psum(back_part.astype(jnp.bfloat16), 'dp').astype(jnp.float32)]
    gather x7 -> x0, local copies, waits for them, and re-layouts: 40.4 us -> none  [the longest x4 18.6 us: pack_rows(): source[owners]]
    dot_general x8 -> x0, matrix products: 33.6 us -> none  [the longest x3 13.3 us: contract_last(): lax.dot_general(left_matrix, right_matrix, (((1,), (1,)), ((), ())), pref...]
    all_to_all x3 -> x0, starting transfers between devices: 27.7 us -> none  [the longest x1 10.8 us: local(): lax.all_to_all(prob_value.astype(jnp.bfloat16).reshape(experts, slot_coun...]
    another operation x3 -> x0, other arithmetic: 18.2 us -> none
  transfers between devices with their start and end apart: 4 -> 0, of which waited for: 3 -> 0; matrix products, arithmetic and copies ran while one was open for 9% -> 0% of each run, Pallas kernels for 0% -> 0%
where the time goes in v1:
time: 183 us; the launch traced here: 181 us
  Pallas kernels  170 us (93%)
  local copies, waits for them, and re-layouts  8.84 us (5%)
  other arithmetic  1.98 us (1%)
    pallas_call x1, Pallas kernels, local(): pl.pallas_call(functools.partial(kernel, lay, steps), out_shape=(sds((n_t...  170 us
    unnamed x9, local copies, waits for them, and re-layouts  8.84 us

profile of v1, /device:TPU:1, one launch (start us, length us, event | category | flops | bytes accessed | tf_op | source)
XLA Modules:
  0.0 181.5 jit_solution(2066288602479265025)
XLA Ops:
  0.6 0.7 convert_bitcast_fusion
  1.3 0.7 convert_bitcast_fusion.1
  2.0 0.6 pad_maximum_fusion.aux
  2.6 170.0 %shard_map.110 = (bf16[128,1024]{1,0:T(8,128)(2,1)}, f32[8,128]{1,0:T(8,128)}, bf16[768,1024]{1,0:T(8,128)(2,1)}, bf16[768,1024]{1,0:T(8,128)(2,1)}, bf16[768,1024]{1,0:T(8,128)(2,1)}) custom-call(bf16[128,1024]{1,0:T(8,128)(2,1)} %tok.1, bf16[128,1024]{1,0:T(8,128)(2,1)} %cot.1, f32[16,128]{1,0:T(8,128)} %pad_maximum_fusion.aux, ...), custom_call_target="tpu_custom_call" | custom-call | tf_op jit(solution)/shard_map/pallas_call | solution.py:656
  172.6 1.7 copy.17
  174.3 1.3 copy.18
  175.5 0.0 copy-start.1
  175.5 2.8 %copy.19 = bf16[1,768,1024]{2,1,0:T(8,128)(2,1)} copy(bf16[1,768,1024]{2,1,0:T(8,128)(2,1)} %bitcast.13) | data formatting | bytes 3145728
  178.3 0.0 copy-done.1
  178.3 0.0 copy-start
  178.3 1.1 copy.20
  179.5 0.8 copy-done
  180.3 1.1 copy.21
Async XLA Ops:
  175.5 2.8 %copy-start.1 = (bf16[768,1024]{1,0:T(8,128)(2,1)S(1)}, bf16[768,1024]{1,0:T(8,128)(2,1)}, u32[]{:S(2)}) copy-start(bf16[768,1024]{1,0:T(8,128)(2,1)} %get-tuple-element.13) | copy-start | bytes 4718596
  178.3 2.0 %copy-start = (bf16[768,1024]{1,0:T(8,128)(2,1)S(1)}, bf16[768,1024]{1,0:T(8,128)(2,1)}, u32[]{:S(2)}) copy-start(bf16[768,1024]{1,0:T(8,128)(2,1)} %get-tuple-element.14) | copy-start | bytes 4718596

commit v2 on v1

--- a/solution.py
+++ b/solution.py
@@ -583,24 +583,23 @@
             ("finish_probs",),
         ]
         return rounds, steps
-    rounds = [([0], False), ([1], False), ([2, -2], False), ([3, 4], True), ([-3], False), ([-1], False)]
+    rounds = [
+        ([0], False), ([1], False), ([2], False), ([3], False), ([4], True), ([-3], False), ([-2], False),
+        ([-1], False),
+    ]
     steps = [
-        ("aux_send",), ("z_send", 1), ("own_wait",), ("gather", 0),
-        ("project", 0), ("fold", 0),
-        ("z_wait", 1), ("z_send", 2), ("gather", 1), ("gather", -1),
-        ("activate", 0), ("relay", 0),
-        ("z_wait", 2), ("z_send", 3), ("gather", 2), ("gather", -2),
-        ("project", 1), ("send_back", 0), ("fold", 1), ("activate", 1),
-        ("z_wait", 3), ("z_send", 4), ("gather", 3), ("gather", -3), ("relay", 1),
-        ("project", 2), ("send_back", 1), ("fold", 2),
-        ("z_wait", 4), ("gather", 4), ("gather_spare",),
-        ("activate", 2), ("project", 3), ("relay", 2), ("fold", 3), ("send_back", 2),
-        ("activate", 3), ("project", 4), ("fold", 4), ("relay", 3), ("activate", 4), ("project", 5),
-        ("send_back", 3), ("fold", 5), ("relay", 4), ("scale",), ("activate", 5),
-        ("wait_spare",), ("combine", 4), ("send_back", 4), ("combine", 3),
-        ("relay", 5), ("combine", -3), ("combine", 2), ("combine", -2), ("send_back", 5),
-        ("combine", 1), ("grads_in",), ("combine", -1), ("grads_down",), ("combine", 0),
-        ("finish_probs",),
+        ("aux_send",), ("z_send", 1), ("own_wait",), ("gather", 0), ("project", 0), ("z_wait", 1),
+        ("z_send", 2), ("fold", 0), ("gather", 1), ("activate", 0), ("gather", -1), ("project", 1),
+        ("z_wait", 2), ("z_send", 3), ("gather", 2), ("fold", 1), ("gather", -2), ("activate", 1),
+        ("project", 2), ("relay", 0), ("z_wait", 3), ("z_send", 4), ("gather", 3), ("fold", 2),
+        ("project", 6), ("gather", -3), ("project", 7), ("activate", 2), ("project", 3), ("z_wait", 4),
+        ("gather", 4), ("relay", 2), ("gather_spare",), ("fold", 3), ("project", 5), ("activate", 3),
+        ("fold", 5), ("project", 4), ("relay", 3), ("scale",), ("fold", 4), ("activate", 5),
+        ("activate", 4), ("send_back", 2), ("send_back", 0), ("relay", 5), ("send_back", 3), ("relay", 4),
+        ("fold", 6), ("relay", 1), ("send_back", 4), ("activate", 6), ("send_back", 5), ("fold", 7),
+        ("wait_spare",), ("combine", 4), ("send_back", 1), ("relay", 6), ("activate", 7), ("combine", 3),
+        ("combine", -3), ("send_back", 6), ("relay", 7), ("combine", 2), ("combine", -2), ("send_back", 7),
+        ("grads_in",), ("combine", 1), ("combine", -1), ("grads_down",), ("combine", 0), ("finish_probs",),
     ]
     return rounds, steps
 

time: 183 us -> 161 us (0.88)
  Pallas kernels: 170 us -> 149 us
    pallas_call x1, Pallas kernels: 170 us -> 149 us  [local(): pl.pallas_call(functools.partial(kernel, lay, steps), out_shape=(sds((n_t...]
where the time goes in v2:
time: 161 us
  Pallas kernels  149 us (93%)
  local copies, waits for them, and re-layouts  8.84 us (5%)
  other arithmetic  1.98 us (1%)
    pallas_call x1, Pallas kernels, local(): pl.pallas_call(functools.partial(kernel, lay, steps), out_shape=(sds((n_t...  149 us
    unnamed x9, local copies, waits for them, and re-layouts  8.84 us

profile of v2, /device:TPU:1, one launch (start us, length us, event | category | flops | bytes accessed | tf_op | source)
XLA Modules:
  0.0 160.9 jit_solution(10168324243828119748)
XLA Ops:
  0.6 0.7 convert_bitcast_fusion
  1.3 0.7 convert_bitcast_fusion.1
  2.0 0.6 pad_maximum_fusion.aux
  2.6 149.4 %shard_map.110 = (bf16[128,1024]{1,0:T(8,128)(2,1)}, f32[8,128]{1,0:T(8,128)}, bf16[768,1024]{1,0:T(8,128)(2,1)}, bf16[768,1024]{1,0:T(8,128)(2,1)}, bf16[768,1024]{1,0:T(8,128)(2,1)}) custom-call(bf16[128,1024]{1,0:T(8,128)(2,1)} %tok.1, bf16[128,1024]{1,0:T(8,128)(2,1)} %cot.1, f32[16,128]{1,0:T(8,128)} %pad_maximum_fusion.aux, ...), custom_call_target="tpu_custom_call" | custom-call | tf_op jit(solution)/shard_map/pallas_call | solution.py:655
  152.0 1.7 %copy.17 = bf16[128,1024]{1,0:T(8,128)(2,1)} copy(bf16[128,1024]{1,0:T(8,128)(2,1)} %get-tuple-element.20) | data formatting | bytes 524288
  153.7 1.3 copy.18
  155.0 0.0 copy-start.1
  155.0 2.8 %copy.19 = bf16[1,768,1024]{2,1,0:T(8,128)(2,1)} copy(bf16[1,768,1024]{2,1,0:T(8,128)(2,1)} %bitcast.13) | data formatting | bytes 3145728
  157.7 0.0 copy-done.1
  157.8 0.0 copy-start
  157.8 1.1 copy.20
  158.9 0.8 copy-done
  159.7 1.1 copy.21
Async XLA Ops:
  155.0 2.8 %copy-start.1 = (bf16[768,1024]{1,0:T(8,128)(2,1)S(1)}, bf16[768,1024]{1,0:T(8,128)(2,1)}, u32[]{:S(2)}) copy-start(bf16[768,1024]{1,0:T(8,128)(2,1)} %get-tuple-element.13) | copy-start | bytes 4718596
  157.8 2.0 %copy-start = (bf16[768,1024]{1,0:T(8,128)(2,1)S(1)}, bf16[768,1024]{1,0:T(8,128)(2,1)}, u32[]{:S(2)}) copy-start(bf16[768,1024]{1,0:T(8,128)(2,1)} %get-tuple-element.14) | copy-start | bytes 4718596
